TPU v7x, 32 devices: a whole 2x2x4 slice. The times are simulated.
32 devices in a mesh: cuts: 4 (over x, core), fiber: 8 (over z, y).
Axes of the slice: x: 2, y: 2, z: 4, core: 2. Of those that a mesh axis runs over, the one named last changes fastest.
Arguments:
- tile_vals: bfloat16 [131072, 128], P(('cuts', 'fiber')), may hold values from -6 to 6
- tile_count: int32 [131072], P(('cuts', 'fiber')), may hold values from 1 to 128
- tile_dest: int32 [131072, 1], P(('cuts', 'fiber')), may hold values from 0 to 3; in each aligned block of 4096 rows (0 to 4095, 4096 to 8191, ...) at most 2048 rows name the same one
- tile_row: int32 [131072], P(('cuts', 'fiber')), may hold values from 0 to 1023, as said below
- tile_block: int32 [131072], P(('cuts', 'fiber')), may hold values from 0 to 3
- tile_first: int32 [131072], P(('cuts', 'fiber')), may hold values from 0 to 255
- factor_one: bfloat16 [8192, 32], P(('cuts', 'fiber')), may hold values from -1.5 to 1.5
- factor_three: bfloat16 [4096, 32], P('fiber'), may hold values from -0.5 to 0.5
- factor_two: bfloat16 [4096, 32], P(('cuts', 'fiber')), may hold values from -0.09375 to 0.09375
Outputs:
- ttmc: bfloat16 [4096, 1024], P(('cuts', 'fiber'))
- projected: float32 [4096, 32], P(('cuts', 'fiber'))
Inputs may be any that keep to these rules, and one draw needn't show every extreme that they name: `tile_dest`: among the tiles of one device, each index of cuts is named at most 2048 times, and exactly 2048 times by some. `tile_row`: among the tiles of one device, each block of 128 consecutive values (starting at multiples of 128) is taken exactly 512 times.
All inputs are finite; a program needn't handle non-finite values.
Results may differ from a plain program's by a relative error of at most 0.002.
Values may be sent and summed in bfloat16 or wider, within the bound.
A program may use at most 128 MiB of HBM per device.

v0:
```python
import jax
import jax.numpy as jnp
from jax import lax
from jax.sharding import PartitionSpec as P

R1 = 32
R3 = 32
FIBER = 128
I2_DEV = 1024


def project_tiles(values, block_ids, factor_three):
    blocks = factor_three.shape[0] // FIBER
    table = factor_three.reshape(blocks, FIBER, R3).transpose(1, 0, 2).reshape(FIBER, blocks * R3)
    every = jnp.dot(values, table, preferred_element_type=jnp.float32).reshape(
        values.shape[0], blocks, R3
    )
    pick = (block_ids[:, None] == jnp.arange(blocks, dtype=jnp.int32)[None, :]).astype(jnp.float32)
    return jnp.sum(every * pick[:, :, None], axis=1)


def slot_of(owners, owner_count, capacity):
    member = (owners[:, None] == jnp.arange(owner_count, dtype=jnp.int32)[None, :]).astype(
        jnp.int32
    )
    before = jnp.cumsum(member, axis=0) - member
    return owners * capacity + jnp.sum(before * member, axis=1)


def place_into(values, slot_ids, owner_count, capacity):
    buffer = jnp.zeros((owner_count * capacity,) + values.shape[1:], values.dtype)
    return buffer.at[slot_ids].set(values).reshape((owner_count, capacity) + values.shape[1:])


def body(
    tile_vals,
    tile_count,
    tile_dest,
    tile_row,
    tile_block,
    tile_first,
    factor_one,
    factor_three,
    factor_two,
):
    ncuts = lax.axis_size("cuts")
    tiles = tile_vals.shape[0]
    positions = jnp.arange(FIBER, dtype=jnp.int32)
    masked = jnp.where(
        positions[None, :] < tile_count[:, None], tile_vals, jnp.zeros_like(tile_vals)
    )
    dest = tile_dest[:, 0]
    first_rows = jnp.take(factor_one, tile_first, axis=0)
    fiber_count = lax.axis_size("fiber")
    block_rows = I2_DEV // fiber_count
    fiber_cap = tiles // fiber_count
    fiber_slots = fiber_count * fiber_cap
    row_owner = tile_row // block_rows
    fiber_slot = slot_of(row_owner, fiber_count, fiber_cap)
    local_proj = project_tiles(masked, tile_block, factor_three)
    first_wide = first_rows.astype(jnp.float32)
    combined = dest * block_rows + tile_row % block_rows
    got_proj, got_first, got_rows = (
        lax.all_to_all(
            place_into(local_proj, fiber_slot, fiber_count, fiber_cap),
            "fiber",
            split_axis=0,
            concat_axis=0,
            tiled=True,
        ),
        lax.all_to_all(
            place_into(first_wide, fiber_slot, fiber_count, fiber_cap),
            "fiber",
            split_axis=0,
            concat_axis=0,
            tiled=True,
        ),
        lax.all_to_all(
            place_into(combined[:, None], fiber_slot, fiber_count, fiber_cap),
            "fiber",
            split_axis=0,
            concat_axis=0,
            tiled=True,
        ),
    )
    proj = got_proj.reshape(fiber_slots, R3)
    first_f = got_first.reshape(fiber_slots, R1)
    target = got_rows.reshape(fiber_slots)
    kron = (first_f[:, :, None] * proj[:, None, :]).reshape(fiber_slots, R1 * R3)
    partial_rows = jax.ops.segment_sum(kron, target, num_segments=ncuts * block_rows)
    summed = lax.psum_scatter(partial_rows, "cuts", scatter_dimension=0, tiled=True)
    ttmc = summed.astype(jnp.bfloat16)
    local_gram = lax.dot_general(
        ttmc, factor_two, (((0,), (0,)), ((), ())), preferred_element_type=jnp.float32
    )
    gram = lax.psum(local_gram, ("cuts", "fiber"))
    gram_b = gram.astype(jnp.bfloat16)
    projected = jnp.dot(ttmc, gram_b, preferred_element_type=jnp.float32) / 32.0
    return (ttmc, projected)


def solution(mesh):
    in_specs = (
        P(("cuts", "fiber"), None),
        P(("cuts", "fiber")),
        P(("cuts", "fiber"), None),
        P(("cuts", "fiber")),
        P(("cuts", "fiber")),
        P(("cuts", "fiber")),
        P(("cuts", "fiber"), None),
        P("fiber", None),
        P(("cuts", "fiber"), None),
    )
    out_specs = (P(("cuts", "fiber"), None), P(("cuts", "fiber"), None))
    return jax.shard_map(body, mesh=mesh, in_specs=in_specs, out_specs=out_specs, check_vma=False)
```

profile of v0, /device:TPU:0, one launch (start us, length us, event | category | flops | bytes accessed | tf_op | source)
XLA Modules:
  0.0 238.0 jit_solution(2505887969231628959)
XLA Ops:
  7.2 0.0 copy-start
  7.2 0.7 broadcast_multiply_fusion.1
  7.9 0.8 reshape.76
  8.7 0.7 fusion.21
  9.4 0.7 fusion.24
  10.2 2.3 reduce-window.6
  12.5 0.3 slice_reduce_fusion
  12.8 0.2 reduce-window.9
  13.0 0.1 add_bitcast_fusion
  13.1 0.1 fusion.18
  13.2 2.2 fusion.3
  15.5 0.0 copy-start.2
  15.5 2.0 copy.31
  17.4 0.0 copy-done.2
  17.5 11.4 %scatter_custom_fusion.2 = f32[4096,32]{1,0:T(8,128)S(1)} fusion(s32[4096]{0:T(1024)S(1)} %get-tuple-element.4, f32[4096,32]{1,0:T(8,128)} %copy.31, f32[]{:T(128)} %constant.50.clone.1), kind=kCustom, calls=%fused_computation.16 | custom fusion | bytes 524800 | tf_op jit(solution)/shard_map/scatter | solution.py:32
  28.9 0.0 copy-start.3
  28.9 1.4 copy.32
  30.3 7.3 %all-to-all-start.2 = ((f32[8,512,32]{1,2,0:T(8,128)}), f32[8,512,32]{1,2,0:T(8,128)S(1)}, u32[]{:S(2)}, u32[]{:S(2)}) async-start(f32[8,512,32]{1,2,0:T(8,128)} %copy.32), calls=%async_computation.2 | async-start | bytes 1048576 | tf_op jit(solution)/shard_map/all_to_all | solution.py:64
  37.6 0.0 copy-done.3
  37.6 0.1 copy.27
  37.7 25.8 %scatter_custom_fusion.1 = f32[4096,32]{1,0:T(8,128)S(1)} fusion(s32[4096]{0:T(1024)S(1)} %get-tuple-element.4, f32[]{:T(128)} %constant.50.clone.1, pred[4096]{0:T(1024)(128)(4,1)S(1)} %compare_and_fusion, bf16[]{:T(256)} %constant.61.clone.1, bf16[256,32]{1,0:T(8,128)(2,1)S(1)} %copy.27, s32[4096]{0:T(1024)S(1)} %get-tuple-element.5), kind=kCustom, calls=%fused_computation.8 | custom fusion | flops 262144 | bytes 610310 | tf_op jit(solution)/shard_map/scatter | solution.py:32
  63.5 1.4 copy.28
  64.9 0.0 all-to-all-done.2
  64.9 6.0 %all-to-all-start.1 = ((f32[8,512,32]{1,2,0:T(8,128)}), f32[8,512,32]{1,2,0:T(8,128)S(1)}, u32[]{:S(2)}, u32[]{:S(2)}) async-start(f32[8,512,32]{1,2,0:T(8,128)} %copy.28), calls=%async_computation.1 | async-start | bytes 1048576 | tf_op jit(solution)/shard_map/all_to_all | solution.py:71
  70.9 16.1 %scatter_custom_fusion = s32[4096]{0:T(1024)} fusion(s32[4096]{0:T(1024)S(1)} %get-tuple-element.4, s32[4096]{0:T(1024)S(1)} %get-tuple-element.2, s32[]{:T(128)} %constant.51.clone.1), kind=kCustom, calls=%fused_computation.51 | custom fusion | bytes 16388 | tf_op jit(solution)/shard_map/scatter | solution.py:32
  87.0 0.0 all-to-all-done.1
  87.0 6.0 %all-to-all-start = ((s32[8,512,1]{1,2,0:T(1,128)}), s32[8,512,1]{1,2,0:T(1,128)S(1)}, u32[]{:S(2)}, u32[]{:S(2)}) async-start(s32[8,512,1]{1,2,0:T(1,128)} %bitcast.3), calls=%async_computation | async-start | bytes 32768 | tf_op jit(solution)/shard_map/all_to_all | solution.py:78
  93.0 0.2 reduce-scatter.2.cloned.1.call-start
  93.3 7.8 %broadcast_multiply_fusion = f32[4096,32,32]{0,2,1:T(8,128)} fusion(f32[4096,32]{0,1:T(8,128)S(1)} %bitcast.53, f32[4096,32]{0,1:T(8,128)S(1)} %bitcast.54), kind=kLoop, calls=%fused_computation.5 | loop fusion | flops 4194304 | bytes 17825792 | tf_op jit(solution)/shard_map/mul | solution.py:89
  101.1 17.5 %copy.34 = f32[4096,1024]{1,0:T(8,128)} copy(f32[4096,1024]{0,1:T(8,128)} %bitcast.50) | data formatting | bytes 33554432 | tf_op jit(solution)/shard_map/mul | solution.py:89
  118.6 0.0 all-to-all-done
  118.6 37.7 %scatter_custom_fusion.3 = f32[512,1024]{1,0:T(8,128)} fusion(s32[4096]{0:T(1024)S(1)} %bitcast.61, f32[4096,1024]{1,0:T(8,128)} %copy.34, f32[]{:T(128)} %constant.50.clone.1), kind=kCustom, calls=%fused_computation.19 | custom fusion | flops 4194304 | bytes 2097664 | tf_op jit(solution)/shard_map/scatter-add | solution.py:90
  156.3 0.0 reduce-scatter.2.cloned.1.call-update
  156.3 32.5 %reduce-scatter.2.cloned.1.call-done = f32[128,1024]{1,0:T(8,128)} async-done(((f32[512,1024]{1,0:T(8,128)}), f32[128,1024]{1,0:T(8,128)}) %reduce-scatter.2.cloned.1.call-update) | async-done | bytes 524304 | tf_op jit(solution)/shard_map/reduce_scatter | solution.py:91
  188.9 1.1 convert_element_type.27
  189.9 0.0 copy-done
  190.0 0.0 copy-start.1
  190.0 0.2 fusion.32
  190.1 40.2 %all-reduce.1 = bf16[1024,32]{0,1:T(8,128)(2,1)S(1)} all-reduce(f32[1024,32]{0,1:T(8,128)S(1)} %fusion.32), channel_id=1, replica_groups=mesh['cuts'=4,'fiber'=8] {'cuts','fiber'}, use_global_device_ids=true, to_apply=%region_9.10 | all-reduce | flops 32768 | bytes 196608 | tf_op jit(solution)/shard_map/psum | solution.py:96
  230.4 0.8 convolution_multiply_fusion.1
  231.2 0.0 copy-done.1
  (5 shorter events, 0.1 us)
Async XLA Ops:
  7.2 182.8 %copy-start = (bf16[128,32]{0,1:T(8,128)(2,1)S(1)}, bf16[128,32]{0,1:T(8,128)(2,1)}, u32[]{:S(2)}) copy-start(bf16[128,32]{0,1:T(8,128)(2,1)} %param.17) | copy-start | bytes 24580
  15.5 2.0 copy-start.2
  28.9 8.7 %copy-start.3 = (bf16[256,32]{0,1:T(8,128)(2,1)S(1)}, bf16[256,32]{0,1:T(8,128)(2,1)}, u32[]{:S(2)}) copy-start(bf16[256,32]{0,1:T(8,128)(2,1)} %param.15) | copy-start | bytes 49156
  30.3 34.6 %all-to-all-start.2 = ((f32[8,512,32]{1,2,0:T(8,128)}), f32[8,512,32]{1,2,0:T(8,128)S(1)}, u32[]{:S(2)}, u32[]{:S(2)}) async-start(f32[8,512,32]{1,2,0:T(8,128)} %copy.32), calls=%async_computation.2 | async-start | bytes 1048576 | tf_op jit(solution)/shard_map/all_to_all | solution.py:64
  64.9 22.1 %all-to-all-start.1 = ((f32[8,512,32]{1,2,0:T(8,128)}), f32[8,512,32]{1,2,0:T(8,128)S(1)}, u32[]{:S(2)}, u32[]{:S(2)}) async-start(f32[8,512,32]{1,2,0:T(8,128)} %copy.28), calls=%async_computation.1 | async-start | bytes 1048576 | tf_op jit(solution)/shard_map/all_to_all | solution.py:71
  87.0 31.5 %all-to-all-start = ((s32[8,512,1]{1,2,0:T(1,128)}), s32[8,512,1]{1,2,0:T(1,128)S(1)}, u32[]{:S(2)}, u32[]{:S(2)}) async-start(s32[8,512,1]{1,2,0:T(1,128)} %bitcast.3), calls=%async_computation | async-start | bytes 32768 | tf_op jit(solution)/shard_map/all_to_all | solution.py:78
  93.0 95.8 %reduce-scatter.2.cloned.1.call-start = ((), (), s32[]{:S(2)}) async-start(), calls=%async_computation.4 | async-start | bytes 2621440 | tf_op jit(solution)/shard_map/reduce_scatter | solution.py:91
  190.0 41.2 %copy-start.1 = (bf16[128,1024]{1,0:T(8,128)(2,1)}, bf16[128,1024]{1,0:T(8,128)(2,1)S(1)}, u32[]{:S(2)}) copy-start(bf16[128,1024]{1,0:T(8,128)(2,1)S(1)} %convert_element_type.27) | copy-start | bytes 786436
Sparse Core Ops, SparseCore 0:
  156.4 32.3 reduce-scatter.1
where the time goes:
time: 239 us; the launch traced here: 238 us
  other arithmetic  77.3 us (32%)
  local copies, waits for them, and re-layouts  51 us (21%)
  blocking collectives  40.2 us (17%)
  waiting for transfers between devices  32.6 us (14%)
  starting transfers between devices  19.5 us (8%)
  between operations  14.2 us (6%)
  matrix products  3.18 us (1%)
    psum x1, blocking collectives, body(): gram = lax.psum(local_gram, ('cuts', 'fiber'))  40.2 us
    scatter-add x1, other arithmetic, body(): jax.ops.segment_sum(kron, target, num_segments=ncuts * block_rows)  37.7 us
    reduce_scatter x1, waiting for transfers between devices, body(): lax.psum_scatter(partial_rows, 'cuts', scatter_dimension=0, tiled=True)  32.5 us
    scatter x2, local copies, waits for them, and re-layouts, place_into(): buffer.at[slot_ids].set(values)  27.5 us
    scatter x1, other arithmetic, place_into(): buffer.at[slot_ids].set(values)  25.8 us
    mul x3, local copies, waits for them, and re-layouts, body(): first_f[:, :, None] * proj[:, None, :]  17.5 us
    mul x1, other arithmetic, body(): first_f[:, :, None] * proj[:, None, :]  7.8 us
    all_to_all x1, starting transfers between devices, body(): lax.all_to_all(place_into(local_proj, fiber_slot, fiber_count, fiber_cap)...  7.31 us
  transfers between devices with their start and end apart: 4, of which 1 were waited for; matrix products, arithmetic and copies ran while one was open for 29% of the time, Pallas kernels for 0%

commit v1 on v0

--- a/solution.py
+++ b/solution.py
@@ -93,7 +93,7 @@
     local_gram = lax.dot_general(
         ttmc, factor_two, (((0,), (0,)), ((), ())), preferred_element_type=jnp.float32
     )
-    gram = lax.psum(local_gram, ("cuts", "fiber"))
+    gram = jnp.sum(lax.all_gather(local_gram, ("cuts", "fiber")), axis=0)
     gram_b = gram.astype(jnp.bfloat16)
     projected = jnp.dot(ttmc, gram_b, preferred_element_type=jnp.float32) / 32.0
     return (ttmc, projected)

time: 239 us -> 268 us (1.12)
  waiting for transfers between devices: 32.6 us -> 96.1 us
  blocking collectives: 40.2 us -> 0 us
  local copies, waits for them, and re-layouts: 51 us -> 55.6 us
    all_gather x0 -> x1, waiting for transfers between devices: none -> 63.6 us  [body(): gram = jnp.sum(lax.all_gather(local_gram, ('cuts', 'fiber')), axis=0)]
    psum x1 -> x0, blocking collectives: 40.2 us -> none  [body(): gram = lax.psum(local_gram, ('cuts', 'fiber'))]
    unnamed x9 -> x10, local copies, waits for them, and re-layouts: 0.15 us -> 4.76 us
  transfers between devices with their start and end apart: 4 -> 5, of which waited for: 1 -> 2; matrix products, arithmetic and copies ran while one was open for 29% -> 26% of each run, Pallas kernels for 0% -> 0%
where the time goes in v1:
time: 268 us; the launch traced here: 267 us
  waiting for transfers between devices  96.1 us (36%)
  other arithmetic  78 us (29%)
  local copies, waits for them, and re-layouts  55.6 us (21%)
  starting transfers between devices  19.6 us (7%)
  between operations  14.2 us (5%)
  matrix products  3.84 us (1%)
    all_gather x1, waiting for transfers between devices, body(): gram = jnp.sum(lax.all_gather(local_gram, ('cuts', 'fiber')), axis=0)  63.6 us
    scatter-add x1, other arithmetic, body(): jax.ops.segment_sum(kron, target, num_segments=ncuts * block_rows)  37.7 us
    reduce_scatter x1, waiting for transfers between devices, body(): lax.psum_scatter(partial_rows, 'cuts', scatter_dimension=0, tiled=True)  32.5 us
    scatter x2, local copies, waits for them, and re-layouts, place_into(): buffer.at[slot_ids].set(values)  27.5 us
    scatter x1, other arithmetic, place_into(): buffer.at[slot_ids].set(values)  25.8 us
    mul x3, local copies, waits for them, and re-layouts, body(): first_f[:, :, None] * proj[:, None, :]  17.5 us
    mul x1, other arithmetic, body(): first_f[:, :, None] * proj[:, None, :]  7.8 us
    all_to_all x1, starting transfers between devices, body(): lax.all_to_all(place_into(local_proj, fiber_slot, fiber_count, fiber_cap)...  7.31 us
  transfers between devices with their start and end apart: 5, of which 2 were waited for; matrix products, arithmetic and copies ran while one was open for 26% of the time, Pallas kernels for 0%

profile of v1, /device:TPU:0, one launch (start us, length us, event | category | flops | bytes accessed | tf_op | source)
XLA Modules:
  0.0 267.3 jit_solution(3690859597496152133)
XLA Ops:
  7.2 0.0 copy-start
  7.2 0.7 broadcast_multiply_fusion.1
  7.9 0.8 reshape.76
  8.7 0.7 fusion.21
  9.4 0.7 fusion.24
  10.2 2.3 reduce-window.6
  12.5 0.3 slice_reduce_fusion
  12.8 0.2 reduce-window.9
  13.0 0.1 add_bitcast_fusion
  13.1 0.1 fusion.18
  13.2 2.2 fusion.3
  15.5 0.0 copy-start.2
  15.5 2.0 copy.31
  17.4 0.0 copy-done.2
  17.5 11.4 %scatter_custom_fusion.2 = f32[4096,32]{1,0:T(8,128)S(1)} fusion(s32[4096]{0:T(1024)S(1)} %get-tuple-element.4, f32[4096,32]{1,0:T(8,128)} %copy.31, f32[]{:T(128)} %constant.50.clone.1), kind=kCustom, calls=%fused_computation.17 | custom fusion | bytes 524800 | tf_op jit(solution)/shard_map/scatter | solution.py:32
  28.9 0.0 copy-start.3
  28.9 1.4 copy.32
  30.3 7.3 %all-to-all-start.2 = ((f32[8,512,32]{1,2,0:T(8,128)}), f32[8,512,32]{1,2,0:T(8,128)S(1)}, u32[]{:S(2)}, u32[]{:S(2)}) async-start(f32[8,512,32]{1,2,0:T(8,128)} %copy.32), calls=%async_computation.2 | async-start | bytes 1048576 | tf_op jit(solution)/shard_map/all_to_all | solution.py:64
  37.6 0.0 copy-done.3
  37.6 0.1 copy.27
  37.7 25.8 %scatter_custom_fusion.1 = f32[4096,32]{1,0:T(8,128)S(1)} fusion(s32[4096]{0:T(1024)S(1)} %get-tuple-element.4, f32[]{:T(128)} %constant.50.clone.1, pred[4096]{0:T(1024)(128)(4,1)S(1)} %compare_and_fusion, bf16[]{:T(256)} %constant.61.clone.1, bf16[256,32]{1,0:T(8,128)(2,1)S(1)} %copy.27, s32[4096]{0:T(1024)S(1)} %get-tuple-element.5), kind=kCustom, calls=%fused_computation.9 | custom fusion | flops 262144 | bytes 610310 | tf_op jit(solution)/shard_map/scatter | solution.py:32
  63.5 1.4 copy.28
  64.9 0.0 all-to-all-done.2
  64.9 6.0 %all-to-all-start.1 = ((f32[8,512,32]{1,2,0:T(8,128)}), f32[8,512,32]{1,2,0:T(8,128)S(1)}, u32[]{:S(2)}, u32[]{:S(2)}) async-start(f32[8,512,32]{1,2,0:T(8,128)} %copy.28), calls=%async_computation.1 | async-start | bytes 1048576 | tf_op jit(solution)/shard_map/all_to_all | solution.py:71
  70.9 16.1 %scatter_custom_fusion = s32[4096]{0:T(1024)} fusion(s32[4096]{0:T(1024)S(1)} %get-tuple-element.4, s32[4096]{0:T(1024)S(1)} %get-tuple-element.2, s32[]{:T(128)} %constant.51.clone.1), kind=kCustom, calls=%fused_computation.52 | custom fusion | bytes 16388 | tf_op jit(solution)/shard_map/scatter | solution.py:32
  87.0 0.0 all-to-all-done.1
  87.0 6.0 %all-to-all-start = ((s32[8,512,1]{1,2,0:T(1,128)}), s32[8,512,1]{1,2,0:T(1,128)S(1)}, u32[]{:S(2)}, u32[]{:S(2)}) async-start(s32[8,512,1]{1,2,0:T(1,128)} %bitcast.3), calls=%async_computation | async-start | bytes 32768 | tf_op jit(solution)/shard_map/all_to_all | solution.py:78
  93.0 0.2 reduce-scatter.2.cloned.1.call-start
  93.3 7.8 %broadcast_multiply_fusion = f32[4096,32,32]{0,2,1:T(8,128)} fusion(f32[4096,32]{0,1:T(8,128)S(1)} %bitcast.59, f32[4096,32]{0,1:T(8,128)S(1)} %bitcast.60), kind=kLoop, calls=%fused_computation.5 | loop fusion | flops 4194304 | bytes 17825792 | tf_op jit(solution)/shard_map/mul | solution.py:89
  101.1 17.5 %copy.34 = f32[4096,1024]{1,0:T(8,128)} copy(f32[4096,1024]{0,1:T(8,128)} %bitcast.55) | data formatting | bytes 33554432 | tf_op jit(solution)/shard_map/mul | solution.py:89
  118.6 0.0 all-to-all-done
  118.6 37.7 %scatter_custom_fusion.3 = f32[512,1024]{1,0:T(8,128)} fusion(s32[4096]{0:T(1024)S(1)} %bitcast.67, f32[4096,1024]{1,0:T(8,128)} %copy.34, f32[]{:T(128)} %constant.50.clone.1), kind=kCustom, calls=%fused_computation.20 | custom fusion | flops 4194304 | bytes 2097664 | tf_op jit(solution)/shard_map/scatter-add | solution.py:90
  156.3 0.0 reduce-scatter.2.cloned.1.call-update
  156.3 0.0 all-gather.3.cloned.1.call-start
  156.4 32.5 %reduce-scatter.2.cloned.1.call-done = f32[128,1024]{1,0:T(8,128)} async-done(((f32[512,1024]{1,0:T(8,128)}), f32[128,1024]{1,0:T(8,128)}) %reduce-scatter.2.cloned.1.call-update) | async-done | bytes 524304 | tf_op jit(solution)/shard_map/reduce_scatter | solution.py:91
  188.9 1.1 convert_element_type.27
  189.9 0.0 copy-done
  190.0 0.0 copy-start.1
  190.0 0.8 fusion.32
  190.8 0.0 all-gather.3.cloned.1.call-update
  190.8 63.6 %all-gather.3.cloned.1.call-done = f32[32768,32]{0,1:T(8,128)} async-done(((f32[1024,32]{0,1:T(8,128)}), f32[32768,32]{0,1:T(8,128)}) %all-gather.3.cloned.1.call-update) | async-done | bytes 4194320 | tf_op jit(solution)/shard_map/all_gather | solution.py:96
  254.4 4.6 %copy.38 = f32[4,8,32,1024]{3,2,1,0:T(8,128)S(1)} copy(f32[4,8,32,1024]{3,1,2,0:T(8,128)} %bitcast.58) | data formatting | bytes 8388608
  259.0 0.6 bitcast_reduce_fusion
  259.6 0.0 copy-done.1
  259.6 0.8 convolution_multiply_fusion.1
  (5 shorter events, 0.1 us)
Async XLA Ops:
  7.2 182.8 %copy-start = (bf16[128,32]{0,1:T(8,128)(2,1)S(1)}, bf16[128,32]{0,1:T(8,128)(2,1)}, u32[]{:S(2)}) copy-start(bf16[128,32]{0,1:T(8,128)(2,1)} %param.17) | copy-start | bytes 24580
  15.5 2.0 copy-start.2
  28.9 8.7 %copy-start.3 = (bf16[256,32]{0,1:T(8,128)(2,1)S(1)}, bf16[256,32]{0,1:T(8,128)(2,1)}, u32[]{:S(2)}) copy-start(bf16[256,32]{0,1:T(8,128)(2,1)} %param.15) | copy-start | bytes 49156
  30.3 34.6 %all-to-all-start.2 = ((f32[8,512,32]{1,2,0:T(8,128)}), f32[8,512,32]{1,2,0:T(8,128)S(1)}, u32[]{:S(2)}, u32[]{:S(2)}) async-start(f32[8,512,32]{1,2,0:T(8,128)} %copy.32), calls=%async_computation.2 | async-start | bytes 1048576 | tf_op jit(solution)/shard_map/all_to_all | solution.py:64
  64.9 22.1 %all-to-all-start.1 = ((f32[8,512,32]{1,2,0:T(8,128)}), f32[8,512,32]{1,2,0:T(8,128)S(1)}, u32[]{:S(2)}, u32[]{:S(2)}) async-start(f32[8,512,32]{1,2,0:T(8,128)} %copy.28), calls=%async_computation.1 | async-start | bytes 1048576 | tf_op jit(solution)/shard_map/all_to_all | solution.py:71
  87.0 31.5 %all-to-all-start = ((s32[8,512,1]{1,2,0:T(1,128)}), s32[8,512,1]{1,2,0:T(1,128)S(1)}, u32[]{:S(2)}, u32[]{:S(2)}) async-start(s32[8,512,1]{1,2,0:T(1,128)} %bitcast.3), calls=%async_computation | async-start | bytes 32768 | tf_op jit(solution)/shard_map/all_to_all | solution.py:78
  93.0 95.8 %reduce-scatter.2.cloned.1.call-start = ((), (), s32[]{:S(2)}) async-start(), calls=%async_computation.4 | async-start | bytes 2621440 | tf_op jit(solution)/shard_map/reduce_scatter | solution.py:91
  156.3 98.0 %all-gather.3.cloned.1.call-start = ((), (), s32[]{:S(2)}) async-start(), calls=%async_computation.5 | async-start | bytes 4325376 | tf_op jit(solution)/shard_map/all_gather | solution.py:96
  190.0 69.7 %copy-start.1 = (bf16[128,1024]{1,0:T(8,128)(2,1)}, bf16[128,1024]{1,0:T(8,128)(2,1)S(1)}, u32[]{:S(2)}) copy-start(bf16[128,1024]{1,0:T(8,128)(2,1)S(1)} %convert_element_type.27) | copy-start | bytes 786436
Sparse Core Ops, SparseCore 0:
  156.4 32.3 reduce-scatter.1
  191.9 62.4 all-gather.2
